TPU v7x, 256 devices: a whole 4x4x8 slice. The times are simulated.
256 devices in a mesh: strata: 16 (over z_lo, x), users: 16 (over y, z_hi, core).
Axes of the slice: x: 4, y: 4, z: 8 (z_hi: 2, z_lo: 4; z = z_hi * 4 + z_lo), core: 2. Of those that a mesh axis runs over, the one named last changes fastest.
Arguments:
- user_factors: float32 [524288, 256], P(('strata', 'users')), may hold values from -1.5 to 1.5
- item_factors: float32 [16384, 256], P(('strata', 'users')), may hold values from -1.5 to 1.5
- tile_rows: int32 [16, 16, 2, 64], P('strata', 'users'), may hold values from 0 to 15, as said below
- tile_columns: int32 [16, 16, 2, 64], P('strata', 'users'), may hold values from 0 to 7, as said below
- tile_counts: int32 [16, 16, 2], P('strata', 'users'), may hold values from 8 to 64, as said below
- ratings: int32 [16, 16, 2, 64, 128, 128], P('strata', 'users'), may hold values from 0 to 5
Outputs:
- updated_users: float32 [524288, 256], P(('strata', 'users'))
- updated_items: float32 [16384, 256], P(('strata', 'users'))
Inputs may be any that keep to these rules, and one draw needn't show every extreme that they name: `tile_rows`: row tile of each slot within the device's users. `tile_columns`: item tile of each slot within the step's item block; a device's slots of one step name distinct pairs of user tile and item tile, padding slots included. `tile_counts`: in every step some device uses all 64 slots.
All inputs are finite; a program needn't handle non-finite values.
Results may differ from a plain program's by a relative error of at most 0.0004.
Values may be sent and summed in bfloat16 or wider, within the bound.
A program may use at most 128 MiB of HBM per device.

v0:
```python
import jax
import jax.numpy as jnp
from jax import lax
from jax.sharding import PartitionSpec as P


def from_behind(block, axis, distance):
    devices = range(lax.axis_size(axis))
    route = [((i - distance) % len(devices), i) for i in devices]
    return lax.ppermute(block, axis, route)


def gradients(user_low, block_low, row_blocks, column_blocks, count, rating_tiles):
    tile_size = rating_tiles.shape[-1]
    factor_width = user_low.shape[1]
    row_tiles = user_low.shape[0] // tile_size
    item_tiles = block_low.shape[0] // tile_size
    slot_count = row_blocks.shape[0]
    user_tiles = user_low.reshape(row_tiles, tile_size, factor_width)[row_blocks]
    item_tiles_now = block_low.reshape(item_tiles, tile_size, factor_width)[column_blocks]
    predicted = jnp.einsum(
        "mik,mjk->mij", user_tiles, item_tiles_now, preferred_element_type=jnp.float32
    )
    in_list = jnp.arange(slot_count) < count
    observed = (rating_tiles > 0) & in_list[:, None, None]
    residual = jnp.where(observed, rating_tiles.astype(jnp.float32) - predicted, 0.0).astype(
        jnp.bfloat16
    )
    user_terms = jnp.einsum(
        "mij,mjk->mik", residual, item_tiles_now, preferred_element_type=jnp.float32
    )
    item_terms = jnp.einsum(
        "mij,mik->mjk", residual, user_tiles, preferred_element_type=jnp.float32
    )
    row_select = (row_blocks[:, None] == jnp.arange(row_tiles)[None, :]).astype(jnp.float32)
    column_select = (column_blocks[:, None] == jnp.arange(item_tiles)[None, :]).astype(jnp.float32)
    user_grad = jnp.einsum("mr,mik->rik", row_select, user_terms, precision=lax.Precision.HIGHEST)
    item_grad = jnp.einsum(
        "mr,mik->rik", column_select, item_terms, precision=lax.Precision.HIGHEST
    )
    return (user_grad.reshape(-1, factor_width), item_grad.reshape(-1, factor_width))


def shards(user_factors, item_factors, tile_rows, tile_columns, tile_counts, ratings):
    row_lists = tile_rows[0, 0]
    column_lists = tile_columns[0, 0]
    count_lists = tile_counts[0, 0]
    rating_lists = ratings[0, 0]
    step_total = rating_lists.shape[0]
    users_now = user_factors
    held_items = lax.all_gather(item_factors, "users", axis=0, tiled=True)
    for step_index in range(step_total):
        user_grad, item_grad = gradients(
            users_now.astype(jnp.bfloat16),
            held_items.astype(jnp.bfloat16),
            row_lists[step_index],
            column_lists[step_index],
            count_lists[step_index],
            rating_lists[step_index],
        )
        summed_grads = lax.psum(item_grad, "users")
        users_now = users_now + 0.01 * (user_grad - 0.05 * users_now)
        held_items = held_items + 0.003 * (summed_grads - 0.05 * held_items)
        if step_index < step_total - 1:
            held_items = from_behind(held_items, "strata", 1)
    own_rows = item_factors.shape[0]
    items_out = lax.dynamic_slice_in_dim(
        held_items, lax.axis_index("users") * own_rows, own_rows, 0
    )
    return (users_now, items_out)


def solution(mesh):
    placed = (
        P(("strata", "users"), None),
        P(("strata", "users"), None),
        P("strata", "users", None, None),
        P("strata", "users", None, None),
        P("strata", "users", None),
        P("strata", "users", None, None, None, None),
    )
    return jax.shard_map(
        shards,
        mesh=mesh,
        in_specs=placed,
        out_specs=(P(("strata", "users"), None), P(("strata", "users"), None)),
        check_vma=False,
    )
```

profile of v0, /device:TPU:1, one launch (start us, length us, event | category | flops | bytes accessed | tf_op | source)
XLA Modules:
  0.0 504.5 jit_solution(3911407407354205349)
XLA Ops:
  7.9 1.7 convert_element_type.36
  10.4 2.8 gather_fusion
  14.5 56.1 %all-gather.2.cloned.1.call-done = f32[1024,256]{1,0:T(8,128)} async-done(((f32[64,256]{1,0:T(8,128)}), f32[1024,256]{1,0:T(8,128)}) %all-gather.2.cloned.1.call-update) | async-done | bytes 1048592 | tf_op jit(solution)/shard_map/all_gather | solution.py:51
  71.9 2.8 gather_fusion.1
  74.7 6.1 %fusion.11 = bf16[64,128,128]{2,1,0:T(8,128)(2,1)S(1)} fusion(s32[1,1,2,64,128,128]{5,4,3,2,1,0:T(8,128)} %param.11, bf16[64,128,256]{2,1,0:T(8,128)(2,1)} %gather_fusion, bf16[64,128,256]{2,1,0:T(8,128)(2,1)} %gather_fusion.1, pred[64]{0:T(512)(128)(4,1)S(1)} %iota_compare_fusion.5), kind=kOutput, calls=%fused_computation.17 | convolution fusion | flops 543162368 | bytes 14680128 | tf_op jit(solution)/shard_map/mik,mjk->mij/dot_general | solution.py:21
  82.1 7.5 %fusion.4 = f32[8,128,256]{2,0,1:T(8,128)S(1)} fusion(f32[64,128,256]{2,1,0:T(8,128)S(1)} %fusion.37, s32[64]{0:T(128)S(1)} %get-tuple-element.3), kind=kOutput, calls=%fused_computation.8 | convolution fusion | flops 201327104 | bytes 9437440 | tf_op jit(solution)/shard_map/mr,mik->rik/dot_general | solution.py:38
  90.9 12.9 %all-reduce.5.cloned.1.call-start = ((), (), s32[]{:S(2)}) async-start(), calls=%async_computation.2 | async-start | bytes 2097152 | tf_op jit(solution)/shard_map/psum | solution.py:61
  104.5 6.8 %fusion.36 = f32[64,128,256]{2,1,0:T(8,128)} fusion(bf16[64,128,128]{2,1,0:T(8,128)(2,1)S(1)} %fusion.11, bf16[64,128,256]{2,1,0:T(8,128)(2,1)} %gather_fusion.1), kind=kOutput, calls=%fused_computation.62 | convolution fusion | flops 536870912 | bytes 14680064 | tf_op jit(solution)/shard_map/mij,mjk->mik/dot_general | solution.py:29
  111.3 155.3 %all-reduce.3.cloned.1.call-done = f32[1024,256]{1,0:T(8,128)} async-done(((f32[1024,256]{1,0:T(8,128)}), f32[1024,256]{1,0:T(8,128)}) %all-reduce.3.cloned.1.call-update) | async-done | bytes 1048592 | tf_op jit(solution)/shard_map/psum | solution.py:61
  266.6 2.4 multiply_add_fusion
  269.0 1.4 collective-permute-start
  270.4 10.7 %fusion.6 = f32[16,128,256]{2,0,1:T(8,128)S(1)} fusion(f32[64,128,256]{2,1,0:T(8,128)} %fusion.36, s32[64]{0:T(128)S(1)} %get-tuple-element.5), kind=kOutput, calls=%fused_computation.10 | convolution fusion | flops 402654208 | bytes 10486016 | tf_op jit(solution)/shard_map/mr,mik->rik/dot_general | solution.py:37
  282.3 1.3 copy-done.4
  284.1 2.8 gather_fusion.2
  286.8 9.7 %collective-permute-done = f32[1024,256]{1,0:T(8,128)} collective-permute-done((f32[1024,256]{1,0:T(8,128)}, f32[1024,256]{1,0:T(8,128)}, u32[]{:S(2)}, u32[]{:S(2)}) %collective-permute-start) | collective-permute-done | bytes 1048608 | tf_op jit(solution)/shard_map/ppermute | solution.py:10
  297.8 2.8 gather_fusion.3
  300.6 6.1 %fusion.9 = bf16[64,128,128]{2,1,0:T(8,128)(2,1)S(1)} fusion(s32[1,1,2,64,128,128]{5,4,3,2,1,0:T(8,128)} %param.11, bf16[64,128,256]{2,1,0:T(8,128)(2,1)} %gather_fusion.2, bf16[64,128,256]{2,1,0:T(8,128)(2,1)} %gather_fusion.3, pred[64]{0:T(512)(128)(4,1)S(1)} %iota_compare_fusion.4), kind=kOutput, calls=%fused_computation.14 | convolution fusion | flops 543162368 | bytes 14680128 | tf_op jit(solution)/shard_map/mik,mjk->mij/dot_general | solution.py:21
  308.9 4.5 fusion.38
  313.4 7.7 %fusion = f32[8,128,256]{2,0,1:T(8,128)S(1)} fusion(f32[64,128,256]{2,1,0:T(8,128)S(1)} %fusion.39, s32[64]{0:T(128)S(1)} %get-tuple-element.2), kind=kOutput, calls=%fused_computation.4 | convolution fusion | flops 201327104 | bytes 9437440 | tf_op jit(solution)/shard_map/mr,mik->rik/dot_general | solution.py:38
  321.0 1.3 copy.11
  322.4 10.7 %fusion.2 = f32[16,128,256]{2,0,1:T(8,128)S(1)} fusion(f32[64,128,256]{2,1,0:T(8,128)} %fusion.38, s32[64]{0:T(128)S(1)} %get-tuple-element.4), kind=kOutput, calls=%fused_computation.6 | convolution fusion | flops 402654208 | bytes 10486016 | tf_op jit(solution)/shard_map/mr,mik->rik/dot_general | solution.py:37
  334.7 1.9 fusion.13
  336.5 159.6 %all-reduce.5.cloned.1.call-done = f32[1024,256]{1,0:T(8,128)} async-done(((f32[1024,256]{1,0:T(8,128)}), f32[1024,256]{1,0:T(8,128)}) %all-reduce.5.cloned.1.call-update) | async-done | bytes 1048592 | tf_op jit(solution)/shard_map/psum | solution.py:61
  496.1 1.5 fusion.18
  (42 shorter events, 14.1 us)
Async XLA Ops:
  7.2 63.5 %all-gather.2.cloned.1.call-start = ((), (), s32[]{:S(2)}) async-start(), calls=%async_computation | async-start | bytes 1114112 | tf_op jit(solution)/shard_map/all_gather | solution.py:51
  7.9 258.7 %all-reduce.3.cloned.1.call-start = ((), (), s32[]{:S(2)}) async-start(), calls=%async_computation.1 | async-start | bytes 2097152 | tf_op jit(solution)/shard_map/psum | solution.py:61
  10.4 2.8 copy-start.9
  10.4 4.0 copy-start.7
  74.7 6.1 %copy-start = (bf16[64,128,256]{2,1,0:T(8,128)(2,1)S(1)}, bf16[64,128,256]{2,1,0:T(8,128)(2,1)}, u32[]{:S(2)}) copy-start(bf16[64,128,256]{2,1,0:T(8,128)(2,1)} %gather_fusion) | copy-start | bytes 12582916
  82.1 22.4 %copy-start.8 = (s32[1,1,2,64]{3,2,1,0:T(2,128)S(1)}, s32[1,1,2,64]{3,2,1,0:T(2,128)}, u32[]{:S(2)}) copy-start(s32[1,1,2,64]{3,2,1,0:T(2,128)} %param.8) | copy-start | bytes 1540
  90.9 405.2 %all-reduce.5.cloned.1.call-start = ((), (), s32[]{:S(2)}) async-start(), calls=%async_computation.2 | async-start | bytes 2097152 | tf_op jit(solution)/shard_map/psum | solution.py:61
  104.5 162.1 %copy-start.6 = (f32[1024,256]{1,0:T(8,128)S(1)}, f32[1024,256]{1,0:T(8,128)}, u32[]{:S(2)}) copy-start(f32[1024,256]{1,0:T(8,128)} %all-gather.2.cloned.1.call-done) | copy-start | bytes 3145732
  269.0 27.5 %collective-permute-start = (f32[1024,256]{1,0:T(8,128)}, f32[1024,256]{1,0:T(8,128)}, u32[]{:S(2)}, u32[]{:S(2)}) collective-permute-start(f32[1024,256]{1,0:T(8,128)} %multiply_add_fusion), channel_id=1, source_target_pairs={{240,0},{0,16},{16,32},{32,48},{48,64},{64,80},{80,96},{96,112},{1... | collective-permute-start | bytes 3145736 | tf_op jit(solution)/shard_map/ppermute | solution.py:10
  281.1 2.6 copy-start.3
  282.3 1.3 copy-start.4
  300.6 6.1 %copy-start.1 = (bf16[64,128,256]{2,1,0:T(8,128)(2,1)S(1)}, bf16[64,128,256]{2,1,0:T(8,128)(2,1)}, u32[]{:S(2)}) copy-start(bf16[64,128,256]{2,1,0:T(8,128)(2,1)} %gather_fusion.2) | copy-start | bytes 12582916
  306.7 2.2 copy-start.2
  333.1 1.6 copy-start.5
Sparse Core Ops, SparseCore 0:
  10.7 59.8 all-gather.1
  91.0 175.5 all-reduce.2
  322.5 173.5 all-reduce.4
where the time goes:
time: 513 us; the launch traced here: 505 us
  waiting for transfers between devices  381 us (74%)
  matrix products  62.6 us (12%)
  local copies, waits for them, and re-layouts  19.3 us (4%)
  between operations  14.4 us (3%)
  starting transfers between devices  14.3 us (3%)
  other arithmetic  12.5 us (2%)
    psum x2, waiting for transfers between devices, shards(): summed_grads = lax.psum(item_grad, 'users')  315 us
    all_gather x1, waiting for transfers between devices, shards(): held_items = lax.all_gather(item_factors, 'users', axis=0, tiled=True)  56.1 us
    dot_general x2, matrix products, gradients(): jnp.einsum('mr,mik->rik', row_select, user_terms, precision=lax.Precision...  21.4 us
    dot_general x2, matrix products, gradients(): jnp.einsum('mr,mik->rik', column_select, item_terms, precision=lax.Precis...  15.2 us
    psum x2, starting transfers between devices, shards(): summed_grads = lax.psum(item_grad, 'users')  12.9 us
    dot_general x2, matrix products, gradients(): jnp.einsum('mik,mjk->mij', user_tiles, item_tiles_now, preferred_element_...  12.2 us
    dot_general x2, matrix products, gradients(): jnp.einsum('mij,mjk->mik', residual, item_tiles_now, preferred_element_ty...  11.3 us
  transfers between devices with their start and end apart: 4, of which 4 were waited for; matrix products, arithmetic and copies ran while one was open for 8% of the time, Pallas kernels for 0%

commit v1 on v0

v1 whole, which is shorter than its diff:
```python
import functools

import jax
import jax.numpy as jnp
from jax import lax
from jax.experimental import pallas as pl
from jax.experimental.pallas import tpu as pltpu
from jax.sharding import PartitionSpec as P

STRATA = 16
MESH = pl.DeviceIdType.MESH
F32 = jnp.float32
BF16 = jnp.bfloat16

AG = {
    "z": 0,
    "a_own": 1, "a_far": 2, "a_relay": 3,
    "b_own": 4, "b_far": 5, "b_relay": 6,
    "c0_own": 7, "c0_far": 8,
    "c1_0": 9, "c1_1": 10, "c2_0": 11, "c2_1": 12, "c3_0": 13, "c3_1": 14,
    "next": 15, "master": 16,
}
AG_COUNT = 17
RS_COUNT = 11


def kernel(
    steps, table, users_hbm, items_ref, ratings_hbm, users_out, items_out,
    rate0, rate1, uf, ub, e_ref, g_ref, s_ref, v0, v1, low_ref, master, master_in,
    rc, ry, rz, load_sem, store_sem, ag_send, ag_recv, rs_send, rs_recv,
):
    s = lax.axis_index("strata")
    u = lax.axis_index("users")
    y = u // 4
    zh = (u // 2) % 2
    c = u % 2
    ya = y + 1 - 2 * (y % 2)
    yb = 3 - y
    yo = (y + 2) % 4
    chunk_y = (y, ya, yb, yo)

    def user(yy, zz, cc):
        return yy * 4 + zz * 2 + cc

    behind = (s + STRATA - 1) % STRATA
    ahead = (s + 1) % STRATA
    core_peer = (s, user(y, zh, 1 - c))
    a_peer = (s, user(ya, zh, c))
    b_peer = (s, user(yb, zh, c))
    z_peer = (s, user(y, 1 - zh, c))
    next_peer = (ahead, u)
    next_z_peer = (ahead, user(y, 1 - zh, c))

    rates = (rate0, rate1)
    vs = (v0, v1)
    slots = ratings_hbm.shape[1]
    row_count = uf.shape[0]
    rows = ub.shape[0] // 8

    barrier = pltpu.get_barrier_semaphore()
    peers = (
        core_peer, a_peer, b_peer, z_peer, next_peer, next_z_peer,
        (behind, u), (behind, user(y, 1 - zh, c)),
    )
    for peer in peers:
        pl.semaphore_signal(barrier, inc=1, device_id=peer, device_id_type=MESH)

    load_users = pltpu.make_async_copy(users_hbm, uf, load_sem.at[0])
    load_users.start()
    load_rates = []
    for t in range(steps):
        copy = pltpu.make_async_copy(
            ratings_hbm.at[t], rates[t].at[pl.ds(0, slots)], load_sem.at[1 + t]
        )
        copy.start()
        load_rates.append(copy)
    for t in range(steps):
        rates[t][slots] = jnp.zeros(rates[t].shape[1:], jnp.int32)

    v0[y, zh, c] = items_ref[...].astype(BF16)
    pl.semaphore_wait(barrier, len(peers))

    def send(src, dst, sems, n, peer):
        copy = pltpu.make_async_remote_copy(
            src_ref=src, dst_ref=dst, send_sem=sems[0].at[n], recv_sem=sems[1].at[n],
            device_id=peer, device_id_type=MESH,
        )
        copy.start()
        return copy

    def convert_users():
        load_users.wait()

        def body(i, carry):
            at = pl.ds(pl.multiple_of(i * rows, rows), rows)
            ub[at, :] = uf[at, :].astype(BF16)
            return carry

        lax.fori_loop(0, 8, body, 0)

    def residuals(t, k):
        yy = chunk_y[k]
        width = e_ref.shape[2]

        def body(i, carry):
            at = pl.ds(pl.multiple_of(i * rows, rows), rows)
            v = vs[t][yy].reshape(width, ub.shape[1])
            p = lax.dot_general(
                ub[at, :], v, (((1,), (1,)), ((), ())), preferred_element_type=F32
            )
            tile = rates[t].shape[1]
            for r in range(rows // tile):
                for j in range(width // tile):
                    slot = table[t * 128 + (i * (rows // tile) + r) * 8 + yy * 2 + j]
                    rate = rates[t][slot]
                    part = p[r * tile:(r + 1) * tile, j * tile:(j + 1) * tile]
                    e = jnp.where(rate > 0, rate.astype(F32) - part, 0.0).astype(BF16)
                    e_ref[
                        k, pl.ds(pl.multiple_of(i * rows + r * tile, tile), tile),
                        j * tile:(j + 1) * tile,
                    ] = e
            return carry

        lax.fori_loop(0, 8, body, 0)

    def item_grad(k):
        g = lax.dot_general(
            e_ref[k], ub[...], (((0,), (0,)), ((), ())), preferred_element_type=F32
        )
        g_ref[k] = g.reshape(g_ref.shape[1:])

    def user_update(t, piece, last):
        def body(i, carry):
            at = pl.ds(pl.multiple_of((piece * 2 + i) * rows, rows), rows)
            total = None
            for k in range(4):
                v = vs[t][chunk_y[k]].reshape(e_ref.shape[2], ub.shape[1])
                term = jnp.dot(e_ref[k, at, :], v, preferred_element_type=F32)
                total = term if total is None else total + term
            now = uf[at, :]
            uf[at, :] = now + 0.01 * (total - 0.05 * now)
            return carry

        lax.fori_loop(0, 2, body, 0)
        if last:
            at = pl.ds(piece * 2 * rows, 2 * rows)
            copy = pltpu.make_async_copy(uf.at[at], users_out.at[at], store_sem.at[piece])
            copy.start()
            return copy
        return None

    def low_users(t):
        def body(i, carry):
            at = pl.ds(pl.multiple_of(i * rows, rows), rows)
            ub[at, :] = uf[at, :].astype(BF16)
            return carry

        lax.fori_loop(0, 8, body, 0)

    for t in range(steps):
        last = t == steps - 1
        v = vs[t]
        sems = (ag_send.at[t], ag_recv.at[t])
        sent = []

        def push(name, yy, zz, peer):
            copy = send(v.at[yy, zz, c], v.at[yy, zz, c], sems, AG[name], peer)
            sent.append(copy)
            return copy

        if t == 0:
            far = push("z", y, zh, z_peer)
        else:
            own_copy.wait_recv()
        a_own = push("a_own", y, zh, a_peer)
        b_own = push("b_own", y, zh, b_peer)
        c_own = push("c0_own", y, zh, core_peer)
        if t == 0:
            convert_users()
            load_rates[0].wait()
        far.wait_recv()
        a_far = push("a_far", y, 1 - zh, a_peer)
        b_far = push("b_far", y, 1 - zh, b_peer)
        c_far = push("c0_far", y, 1 - zh, core_peer)
        if t > 0:
            load_rates[t].wait()
        c_own.wait_recv()
        c_far.wait_recv()
        residuals(t, 0)
        a_own.wait_recv()
        a_far.wait_recv()
        a_relay = push("b_relay", ya, 0, b_peer)
        c1 = (push("c1_0", ya, 0, core_peer), push("c1_1", ya, 1, core_peer))
        b_own.wait_recv()
        b_far.wait_recv()
        b_relay = push("a_relay", yb, 1, a_peer)
        c2 = (push("c2_0", yb, 0, core_peer), push("c2_1", yb, 1, core_peer))
        c1[0].wait_recv()
        c1[1].wait_recv()
        residuals(t, 1)
        a_relay.wait_recv()
        c3_0 = push("c3_0", yo, 0, core_peer)
        b_relay.wait_recv()
        c3_1 = push("c3_1", yo, 1, core_peer)
        c2[0].wait_recv()
        c2[1].wait_recv()
        residuals(t, 2)
        c3_0.wait_recv()
        c3_1.wait_recv()
        residuals(t, 3)

        rsems = (rs_send.at[t], rs_recv.at[t])
        out = []

        def over_core(k):
            copy = send(g_ref.at[k, :, 1 - c], rc.at[t, k], rsems, k, core_peer)
            out.append(copy)
            return copy

        def over_y(src, n, peer):
            copy = send(src, ry.at[t, n], rsems, 4 + n, peer)
            out.append(copy)
            return copy

        def core_sum(k, copy):
            copy.wait_recv()
            for z in range(2):
                s_ref[k, z] = g_ref[k, z, c] + rc[t, k, z]

        item_grad(3)
        core3 = over_core(3)
        item_grad(1)
        core1 = over_core(1)
        core_sum(3, core3)
        y0 = over_y(s_ref.at[3, 0], 0, a_peer)
        y1 = over_y(s_ref.at[3, 1], 1, b_peer)
        item_grad(2)
        core2 = over_core(2)
        core_sum(1, core1)
        y2 = over_y(s_ref.at[1, 0], 2, a_peer)
        item_grad(0)
        core0 = over_core(0)
        core_sum(2, core2)
        y3 = over_y(s_ref.at[2, 1], 3, b_peer)
        y0.wait_recv()
        s_ref[2, 0] = s_ref[2, 0] + ry[t, 0]
        y4 = over_y(s_ref.at[2, 0], 4, b_peer)
        y1.wait_recv()
        s_ref[1, 1] = s_ref[1, 1] + ry[t, 1]
        y5 = over_y(s_ref.at[1, 1], 5, a_peer)
        core_sum(0, core0)
        stores = [user_update(t, 0, last)]
        y2.wait_recv()
        y3.wait_recv()
        y4.wait_recv()
        y5.wait_recv()
        s_ref[0, 0] = s_ref[0, 0] + ry[t, 2] + ry[t, 4]
        s_ref[0, 1] = s_ref[0, 1] + ry[t, 3] + ry[t, 5]
        over_z = send(s_ref.at[0, 1 - zh], rz.at[t], rsems, 10, z_peer)
        out.append(over_z)
        for piece in range(1, 4):
            stores.append(user_update(t, piece, last))
        if not last:
            low_users(t)
        if t > 0:
            master_copy.wait_recv()
        over_z.wait_recv()
        grad = s_ref[0, zh] + rz[t]
        now = items_ref[...] if t == 0 else master_in[...]
        now = now + 0.003 * (grad - 0.05 * now)
        if last:
            items_out[...] = now
        else:
            low_ref[...] = now.astype(BF16)
            master[...] = now
            nsems = (ag_send.at[t + 1], ag_recv.at[t + 1])
            dst = vs[t + 1].at[y, zh, c]
            far = send(low_ref, dst, nsems, AG["z"], next_z_peer)
            own_copy = send(low_ref, dst, nsems, AG["next"], next_peer)
            master_copy = send(master, master_in, nsems, AG["master"], next_peer)
            late = [far, own_copy, master_copy]
        for copy in sent + out:
            copy.wait_send()
        for copy in stores:
            if copy is not None:
                copy.wait()
        if last:
            for copy in late:
                copy.wait_send()


def shards(user_factors, item_factors, tile_rows, tile_columns, tile_counts, ratings):
    steps, slots, tile = ratings.shape[2], ratings.shape[3], ratings.shape[4]
    users, width = user_factors.shape
    own = item_factors.shape[0]
    pairs = 128
    pair = tile_rows[0, 0] * 8 + tile_columns[0, 0]
    slot = jnp.arange(slots, dtype=jnp.int32)
    live = slot[None, :] < tile_counts[0, 0][:, None]
    named = (pair[:, None, :] == jnp.arange(pairs)[None, :, None]) & live[:, None, :]
    table = slots + jnp.sum(jnp.where(named, slot - slots, 0), axis=2, dtype=jnp.int32)

    anywhere = pl.BlockSpec(memory_space=pl.ANY)
    vmem = pl.BlockSpec(memory_space=pltpu.VMEM)
    block = (4, 2, 2, own, width)
    return pl.pallas_call(
        functools.partial(kernel, steps),
        out_shape=(
            jax.ShapeDtypeStruct((users, width), F32),
            jax.ShapeDtypeStruct((own, width), F32),
        ),
        in_specs=[pl.BlockSpec(memory_space=pltpu.SMEM), anywhere, vmem, anywhere],
        out_specs=(anywhere, vmem),
        scratch_shapes=[
            pltpu.VMEM((slots + 1, tile, tile), jnp.int32),
            pltpu.VMEM((slots + 1, tile, tile), jnp.int32),
            pltpu.VMEM((users, width), F32),
            pltpu.VMEM((users, width), BF16),
            pltpu.VMEM((4, users, 4 * own), BF16),
            pltpu.VMEM(block, F32),
            pltpu.VMEM((4, 2, own, width), F32),
            pltpu.VMEM(block, BF16),
            pltpu.VMEM(block, BF16),
            pltpu.VMEM((own, width), BF16),
            pltpu.VMEM((own, width), F32),
            pltpu.VMEM((own, width), F32),
            pltpu.VMEM((steps, 4, 2, own, width), F32),
            pltpu.VMEM((steps, 6, own, width), F32),
            pltpu.VMEM((steps, own, width), F32),
            pltpu.SemaphoreType.DMA((1 + steps,)),
            pltpu.SemaphoreType.DMA((4,)),
            pltpu.SemaphoreType.DMA((steps, AG_COUNT)),
            pltpu.SemaphoreType.DMA((steps, AG_COUNT)),
            pltpu.SemaphoreType.DMA((steps, RS_COUNT)),
            pltpu.SemaphoreType.DMA((steps, RS_COUNT)),
        ],
        compiler_params=pltpu.CompilerParams(
            collective_id=0, has_side_effects=True, vmem_limit_bytes=56 << 20
        ),
        name="sgd_steps",
    )(table.reshape(-1), user_factors, item_factors, ratings[0, 0])


def solution(mesh):
    placed = (
        P(("strata", "users"), None),
        P(("strata", "users"), None),
        P("strata", "users", None, None),
        P("strata", "users", None, None),
        P("strata", "users", None),
        P("strata", "users", None, None, None, None),
    )
    return jax.shard_map(
        shards,
        mesh=mesh,
        in_specs=placed,
        out_specs=(P(("strata", "users"), None), P(("strata", "users"), None)),
        check_vma=False,
    )
```

time: 513 us -> 80.2 us (0.16); the launches traced: 505 us -> 78.6 us
  waiting for transfers between devices: 381 us -> 0 us
  Pallas kernels: 0 us -> 72.1 us
  matrix products: 62.6 us -> 0 us
  local copies, waits for them, and re-layouts: 19.3 us -> 3.71 us
  starting transfers between devices: 14.3 us -> 0 us
  between operations: 14.4 us -> 0.65 us
  other arithmetic: 12.5 us -> 2.12 us
    psum x2 -> x0, waiting for transfers between devices: 315 us -> none  [shards(): summed_grads = lax.psum(item_grad, 'users')]
    pallas_call x0 -> x1, Pallas kernels: none -> 72.1 us  [shards(): pl.pallas_call(functools.partial(kernel, steps), out_shape=(jax.ShapeDtyp...]
    dot_general x10 -> x0, matrix products: 62.6 us -> none  [the longest x2 21.4 us: gradients(): jnp.einsum('mr,mik->rik', row_select, user_terms, precision=lax.Precision...]
    all_gather x1 -> x0, waiting for transfers between devices: 56.1 us -> none  [shards(): held_items = lax.all_gather(item_factors, 'users', axis=0, tiled=True)]
    psum x2 -> x0, starting transfers between devices: 12.9 us -> none  [shards(): summed_grads = lax.psum(item_grad, 'users')]
    gather x4 -> x0, local copies, waits for them, and re-layouts: 11.1 us -> none  [the longest x2 5.58 us: gradients(): block_low.reshape(item_tiles, tile_size, factor_width)[column_blocks]]
    ppermute x1 -> x0, waiting for transfers between devices: 9.68 us -> none  [from_behind(): return lax.ppermute(block, axis, route)]
  transfers between devices with their start and end apart: 4 -> 0, of which waited for: 4 -> 0; matrix products, arithmetic and copies ran while one was open for 8% -> 0% of each run, Pallas kernels for 0% -> 0%
where the time goes in v1:
time: 80.2 us; the launch traced here: 78.6 us
  Pallas kernels  72.1 us (90%)
  local copies, waits for them, and re-layouts  3.71 us (5%)
  other arithmetic  2.12 us (3%)
    pallas_call x1, Pallas kernels, shards(): pl.pallas_call(functools.partial(kernel, steps), out_shape=(jax.ShapeDtyp...  72.1 us
    unnamed x4, local copies, waits for them, and re-layouts  3.71 us

profile of v1, /device:TPU:1, one launch (start us, length us, event | category | flops | bytes accessed | tf_op | source)
XLA Modules:
  0.0 78.6 jit_solution(5812555803279184386)
XLA Ops:
  0.6 0.7 iota_compare_fusion.1
  1.4 0.7 add_bitcast_fusion.1
  2.1 0.1 select_reduce_fusion
  2.2 0.6 add_bitcast_fusion.table
  2.8 72.1 %sgd_steps.1 = (f32[2048,256]{1,0:T(8,128)}, f32[64,256]{1,0:T(8,128)}) custom-call(s32[256]{0:T(256)} %add_bitcast_fusion.table, f32[2048,256]{1,0:T(8,128)} %users_hbm.1, f32[64,256]{1,0:T(8,128)} %items_ref.1, s32[2,64,128,128]{3,2,1,0:T(8,128)} %bitcast.6), custom_call_target="tpu_custom_call" | custom-call | tf_op jit(solution)/shard_map/sgd_steps/pallas_call | solution.py:306
  74.9 0.0 copy-start
  74.9 3.1 %copy.10 = f32[2048,256]{1,0:T(8,128)} copy(f32[2048,256]{1,0:T(8,128)} %get-tuple-element.4) | data formatting | bytes 4194304
  78.0 0.0 copy-done
  78.0 0.6 copy.11
  (1 shorter events, 0.0 us)
Async XLA Ops:
  74.9 3.1 %copy-start = (f32[64,256]{1,0:T(8,128)S(1)}, f32[64,256]{1,0:T(8,128)}, u32[]{:S(2)}) copy-start(f32[64,256]{1,0:T(8,128)} %get-tuple-element.5) | copy-start | bytes 196612

commit v2 on v0

v2 whole, which is shorter than its diff:
```python
import functools

import jax
import jax.numpy as jnp
from jax import lax
from jax.experimental import pallas as pl
from jax.experimental.pallas import tpu as pltpu
from jax.sharding import PartitionSpec as P

STRATA = 16
MESH = pl.DeviceIdType.MESH
F32 = jnp.float32
BF16 = jnp.bfloat16

PAIRS = 128
LIMIT = 32766.0
STEP = 64.0
PAIRS = 128
LIMIT = 32766.0
STEP = 64.0


def encode(x):
    top = jnp.maximum(jnp.max(jnp.abs(x), axis=0, keepdims=True), 1e-30)
    level = jnp.ceil(jnp.log2(top) * STEP)
    code = jnp.round(x * (LIMIT * jnp.exp2(level * (-1.0 / STEP)))).astype(jnp.int32)
    level = jnp.broadcast_to(level.astype(jnp.int32), (16, x.shape[1]))
    return code.astype(jnp.int16), level.astype(jnp.int16)


def decode(ref):
    rows = ref.shape[0] - 16
    level = ref[rows:, :].astype(jnp.int32)[0:1, :].astype(F32)
    scale = jnp.exp2(level * (1.0 / STEP)) * (1.0 / LIMIT)
    return ref[:rows, :].astype(jnp.int32).astype(F32) * scale


def kernel(
    steps, rows_ref, columns_ref, counts_ref, users_hbm, items_ref, ratings_hbm,
    uf, items_out,
    rate0, rate1, ub, e_ref, g_ref, s_ref, v0, v1, master,
    rc, code_out, code_in, shift_out, shift_in, last_out, last_in,
    table_v, table, load_sem, ag_send, ag_recv, rs_send, rs_recv, next_send, next_recv,
):
    s = lax.axis_index("strata")
    u = lax.axis_index("users")
    y = u // 4
    zh = (u // 2) % 2
    c = u % 2
    ya = y + 1 - 2 * (y % 2)
    yb = 3 - y
    yo = (y + 2) % 4
    chunk_y = (y, ya, yb, yo)

    def user(yy, zz, cc):
        return yy * 4 + zz * 2 + cc

    behind = (s + STRATA - 1) % STRATA
    ahead = (s + 1) % STRATA
    y_peers = tuple((s, user(yy, zh, c)) for yy in chunk_y)
    core_peer = (s, user(y, zh, 1 - c))
    z_peer = (s, user(y, 1 - zh, c))
    next_peers = ((ahead, u), (ahead, user(y, 1 - zh, c)))
    peers = (
        core_peer, z_peer, *y_peers[1:], *next_peers,
        (behind, u), (behind, user(y, 1 - zh, c)),
    )

    rates = (rate0, rate1)
    vs = (v0, v1)
    slots, tile = ratings_hbm.shape[1], ratings_hbm.shape[2]
    user_count, width = ub.shape
    own = items_ref.shape[0]
    wide = 4 * own

    barrier = pltpu.get_barrier_semaphore()
    for peer in peers:
        pl.semaphore_signal(barrier, inc=1, device_id=peer, device_id_type=MESH)

    load_users = pltpu.make_async_copy(users_hbm, uf, load_sem.at[0])
    load_users.start()
    load_rates = []
    for t in range(steps):
        copy = pltpu.make_async_copy(
            ratings_hbm.at[t], rates[t].at[pl.ds(0, slots)], load_sem.at[1 + t]
        )
        copy.start()
        load_rates.append(copy)
    for t in range(steps):
        rates[t][slots] = jnp.zeros((tile, tile), jnp.int32)
    v0[y, zh, c] = items_ref[...].astype(BF16)

    def send(src, dst, sems, n, peer):
        copy = pltpu.make_async_remote_copy(
            src_ref=src, dst_ref=dst, send_sem=sems[0].at[n], recv_sem=sems[1].at[n],
            device_id=peer, device_id_type=MESH,
        )
        copy.start()
        return copy

    def low_users(i, carry):
        at = pl.ds(pl.multiple_of(i * 256, 256), 256)
        ub[at, :] = uf[at, :].astype(BF16)
        return carry

    def fill_table():
        lanes = lax.broadcasted_iota(jnp.int32, (1, PAIRS), 1)
        for t in range(steps):
            count = counts_ref[0, 0, t]

            def name(m, found):
                pair = rows_ref[0, 0, t, m] * 8 + columns_ref[0, 0, t, m]
                pair = jnp.where(m < count, pair, -1)
                return jnp.where(lanes == pair, m, found)

            table_v[t:t + 1, :] = lax.fori_loop(
                0, slots, name, jnp.full((1, PAIRS), slots, jnp.int32)
            )
        copy = pltpu.make_async_copy(table_v, table, load_sem.at[1 + steps])
        copy.start()
        copy.wait()

    def residuals(t, k):
        yy = chunk_y[k]
        p = lax.dot_general(
            ub[...], vs[t][yy].reshape(wide, width), (((1,), (1,)), ((), ())),
            preferred_element_type=F32,
        )
        for r in range(user_count // tile):
            for j in range(wide // tile):
                rate = rates[t][table[t, r * 8 + yy * 2 + j]]
                part = p[r * tile:(r + 1) * tile, j * tile:(j + 1) * tile]
                e = jnp.where(rate > 0, rate.astype(F32) - part, 0.0).astype(BF16)
                e_ref[k, r * tile:(r + 1) * tile, j * tile:(j + 1) * tile] = e

    def item_grad(k):
        g = lax.dot_general(
            e_ref[k], ub[...], (((0,), (0,)), ((), ())), preferred_element_type=F32
        )
        g_ref[k] = g.reshape(g_ref.shape[1:])

    def user_update(t, piece):
        at = pl.ds(piece * (user_count // 4), user_count // 4)
        total = None
        for k in range(4):
            v = vs[t][chunk_y[k]].reshape(wide, width)
            term = jnp.dot(e_ref[k, at, :], v, preferred_element_type=F32)
            total = term if total is None else total + term
        now = uf[at, :]
        uf[at, :] = now + 0.01 * (total - 0.05 * now)

    pl.semaphore_wait(barrier, len(peers))

    for t in range(steps):
        last = t == steps - 1
        v = vs[t]
        sems = (ag_send.at[t], ag_recv.at[t])
        sent = []

        def push(part, n, peer):
            copy = send(part, part, sems, n, peer)
            sent.append(copy)
            return copy

        if t == 0:
            far = push(v.at[y, zh, c], 0, z_peer)
            near = [push(v.at[y, zh, c], k, y_peers[k]) for k in (3, 1, 2)]
            core = [push(v.at[y, zh, c], 4, core_peer)]
            load_users.wait()
            lax.fori_loop(0, user_count // 256, low_users, 0)
            fill_table()
            far.wait_recv()
            more = [push(v.at[y, 1 - zh, c], 5 + k, y_peers[k]) for k in (3, 1, 2)]
            core.append(push(v.at[y, 1 - zh, c], 5, core_peer))
            arrivals = {k: [near[i], more[i]] for i, k in enumerate((3, 1, 2))}
        else:
            both = v.at[y, :, c]
            near = [push(both, k, y_peers[k]) for k in (3, 1, 2)]
            core = [push(both, 4, core_peer)]
            arrivals = {k: [near[i]] for i, k in enumerate((3, 1, 2))}
        load_rates[t].wait()
        for copy in core:
            copy.wait_recv()
        residuals(t, 0)
        forward = {}
        for k in (1, 2, 3):
            for copy in arrivals[k]:
                copy.wait_recv()
            forward[k] = push(v.at[chunk_y[k], :, c], 8 + k, core_peer)
            if k > 1:
                forward[k - 1].wait_recv()
                residuals(t, k - 1)
        if t == 0:
            carried = [
                send(items_ref, master.at[zh], (next_send, next_recv), i, next_peers[i])
                for i in range(2)
            ]
        forward[3].wait_recv()
        residuals(t, 3)

        rsems = (rs_send.at[t], rs_recv.at[t])

        def over_core(k):
            item_grad(k)
            copy = send(g_ref.at[k, :, 1 - c], rc.at[t, k], rsems, k, core_peer)
            sent.append(copy)
            return copy

        def core_sum(k, copy):
            copy.wait_recv()
            return (g_ref[k, :, c] + rc[t, k]).reshape(2 * own, width)

        def over_y(k, copy):
            code, level = encode(core_sum(k, copy))
            code_out[t, k - 1, :2 * own] = code
            code_out[t, k - 1, 2 * own:] = level
            copy = send(
                code_out.at[t, k - 1], code_in.at[t, k - 1], rsems, 3 + k, y_peers[k]
            )
            sent.append(copy)
            return copy

        core3 = over_core(3)
        core1 = over_core(1)
        y3 = over_y(3, core3)
        core2 = over_core(2)
        y1 = over_y(1, core1)
        core0 = over_core(0)
        y2 = over_y(2, core2)
        user_update(t, 0)
        s_ref[...] = core_sum(0, core0)
        user_update(t, 1)
        for k, copy in ((3, y3), (1, y1), (2, y2)):
            copy.wait_recv()
            s_ref[...] = s_ref[...] + decode(code_in.at[t, k - 1])
        if not last:
            code, level = encode(s_ref[...])
            shift_out[:2 * own] = code
            shift_out[2 * own:] = level
            shifted = [
                send(shift_out, shift_in.at[zh], (next_send, next_recv), 2 + i, next_peers[i])
                for i in range(2)
            ]
            user_update(t, 2)
            user_update(t, 3)
            lax.fori_loop(0, user_count // 256, low_users, 0)
            for copy in carried + shifted:
                copy.wait_recv()
            grad = decode(shift_in.at[0]) + decode(shift_in.at[1])
            now = master[...].reshape(2 * own, width)
            now = now + 0.003 * (grad - 0.05 * now)
            master[...] = now.reshape(2, own, width)
            vs[t + 1][y, :, c] = now.astype(BF16).reshape(2, own, width)
        else:
            code, level = encode(s_ref[pl.ds(pl.multiple_of((1 - zh) * own, own), own), :])
            last_out[:own] = code
            last_out[own:] = level
            final = send(last_out, last_in, rsems, 7, z_peer)
            sent.append(final)
            user_update(t, 2)
            user_update(t, 3)
            now = master[zh]
            kept = s_ref[pl.ds(pl.multiple_of(zh * own, own), own), :]
            final.wait_recv()
            grad = kept + decode(last_in)
            items_out[...] = now + 0.003 * (grad - 0.05 * now)
        for copy in sent:
            copy.wait_send()
    for copy in carried + shifted:
        copy.wait_send()


def shards(user_factors, item_factors, tile_rows, tile_columns, tile_counts, ratings):
    steps, slots, tile = ratings.shape[2], ratings.shape[3], ratings.shape[4]
    users, width = user_factors.shape
    own = item_factors.shape[0]
    anywhere = pl.BlockSpec(memory_space=pl.ANY)
    vmem = pl.BlockSpec(memory_space=pltpu.VMEM)
    smem = pl.BlockSpec(memory_space=pltpu.SMEM)
    block = (4, 2, 2, own, width)
    coded = 2 * own + 16
    return pl.pallas_call(
        functools.partial(kernel, steps),
        out_shape=(
            pltpu.VMEM((users, width), F32),
            pltpu.VMEM((own, width), F32),
        ),
        in_specs=[smem, smem, smem, anywhere, vmem, anywhere],
        out_specs=(vmem, vmem),
        scratch_shapes=[
            pltpu.VMEM((slots + 1, tile, tile), jnp.int32),
            pltpu.VMEM((slots + 1, tile, tile), jnp.int32),
            pltpu.VMEM((users, width), BF16),
            pltpu.VMEM((4, users, 4 * own), BF16),
            pltpu.VMEM(block, F32),
            pltpu.VMEM((2 * own, width), F32),
            pltpu.VMEM(block, BF16),
            pltpu.VMEM(block, BF16),
            pltpu.VMEM((2, own, width), F32),
            pltpu.VMEM((steps, 4, 2, own, width), F32),
            pltpu.VMEM((steps, 3, coded, width), jnp.int16),
            pltpu.VMEM((steps, 3, coded, width), jnp.int16),
            pltpu.VMEM((coded, width), jnp.int16),
            pltpu.VMEM((2, coded, width), jnp.int16),
            pltpu.VMEM((own + 16, width), jnp.int16),
            pltpu.VMEM((own + 16, width), jnp.int16),
            pltpu.VMEM((steps, PAIRS), jnp.int32),
            pltpu.SMEM((steps, PAIRS), jnp.int32),
            pltpu.SemaphoreType.DMA((2 + steps,)),
            pltpu.SemaphoreType.DMA((steps, 12)),
            pltpu.SemaphoreType.DMA((steps, 12)),
            pltpu.SemaphoreType.DMA((steps, 8)),
            pltpu.SemaphoreType.DMA((steps, 8)),
            pltpu.SemaphoreType.DMA((4,)),
            pltpu.SemaphoreType.DMA((4,)),
        ],
        compiler_params=pltpu.CompilerParams(
            collective_id=0, has_side_effects=True, vmem_limit_bytes=56 << 20
        ),
        name="sgd_steps",
    )(tile_rows, tile_columns, tile_counts, user_factors, item_factors, ratings[0, 0])


def solution(mesh):
    placed = (
        P(("strata", "users"), None),
        P(("strata", "users"), None),
        P("strata", "users", None, None),
        P("strata", "users", None, None),
        P("strata", "users", None),
        P("strata", "users", None, None, None, None),
    )
    return jax.shard_map(
        shards,
        mesh=mesh,
        in_specs=placed,
        out_specs=(P(("strata", "users"), None), P(("strata", "users"), None)),
        check_vma=False,
    )
```

time: 513 us -> 62.5 us (0.12); the launches traced: 505 us -> 62.4 us
  waiting for transfers between devices: 381 us -> 0 us
  matrix products: 62.6 us -> 0 us
  Pallas kernels: 0 us -> 59.8 us
  local copies, waits for them, and re-layouts: 19.3 us -> 1.95 us
  starting transfers between devices: 14.3 us -> 0 us
  between operations: 14.4 us -> 0.64 us
  other arithmetic: 12.5 us -> 0 us
    psum x2 -> x0, waiting for transfers between devices: 315 us -> none  [shards(): summed_grads = lax.psum(item_grad, 'users')]
    dot_general x10 -> x0, matrix products: 62.6 us -> none  [the longest x2 21.4 us: gradients(): jnp.einsum('mr,mik->rik', row_select, user_terms, precision=lax.Precision...]
    pallas_call x0 -> x1, Pallas kernels: none -> 59.8 us  [shards(): pl.pallas_call(functools.partial(kernel, steps), out_shape=(pltpu.VMEM((u...]
    all_gather x1 -> x0, waiting for transfers between devices: 56.1 us -> none  [shards(): held_items = lax.all_gather(item_factors, 'users', axis=0, tiled=True)]
    psum x2 -> x0, starting transfers between devices: 12.9 us -> none  [shards(): summed_grads = lax.psum(item_grad, 'users')]
    gather x4 -> x0, local copies, waits for them, and re-layouts: 11.1 us -> none  [the longest x2 5.58 us: gradients(): block_low.reshape(item_tiles, tile_size, factor_width)[column_blocks]]
    ppermute x1 -> x0, waiting for transfers between devices: 9.68 us -> none  [from_behind(): return lax.ppermute(block, axis, route)]
    add x3 -> x0, other arithmetic: 5.76 us -> none  [the longest x2 3.9 us: shards(): held_items = held_items + 0.003 * (summed_grads - 0.05 * held_items)]
  transfers between devices with their start and end apart: 4 -> 0, of which waited for: 4 -> 0; matrix products, arithmetic and copies ran while one was open for 8% -> 0% of each run, Pallas kernels for 0% -> 0%
where the time goes in v2:
time: 62.5 us; the launch traced here: 62.4 us
  Pallas kernels  59.8 us (96%)
  local copies, waits for them, and re-layouts  1.95 us (3%)
  between operations  0.64 us (1%)
    pallas_call x1, Pallas kernels, shards(): pl.pallas_call(functools.partial(kernel, steps), out_shape=(pltpu.VMEM((u...  59.8 us
    unnamed x2, local copies, waits for them, and re-layouts  1.95 us

profile of v2, /device:TPU:1, one launch (start us, length us, event | category | flops | bytes accessed | tf_op | source)
XLA Modules:
  0.0 62.4 jit_solution(5133387071307129665)
XLA Ops:
  0.6 59.8 %sgd_steps.1 = (f32[2048,256]{1,0:T(8,128)S(1)}, f32[64,256]{1,0:T(8,128)S(1)}) custom-call(s32[1,1,2,64]{3,2,1,0:T(2,128)} %rows_ref.1, s32[1,1,2,64]{3,2,1,0:T(2,128)} %columns_ref.1, s32[1,1,2]{2,1,0:T(1,128)} %counts_ref.1, f32[2048,256]{1,0:T(8,128)} %users_hbm.1, f32[64,256]{1,0:T(8,128)} %items_ref.1, s32[2,64,128,128]{3,2,1,0:T(8,128)} %bitcast.1), custom_call_target="tpu_custom_call" | custom-call | tf_op jit(solution)/shard_map/sgd_steps/pallas_call | solution.py:282
  60.5 1.3 %copy.10 = f32[2048,256]{1,0:T(8,128)} copy(f32[2048,256]{1,0:T(8,128)S(1)} %get-tuple-element.2) | data formatting | bytes 4194304
  61.8 0.6 %copy.11 = f32[64,256]{1,0:T(8,128)} copy(f32[64,256]{1,0:T(8,128)S(1)} %get-tuple-element.3) | data formatting | bytes 131072
